TPU v7x, 256 devices: a whole 4x4x8 slice. The times are simulated.
256 devices in a mesh: gx: 8 (over y, z_hi), gy: 8 (over x, core), gz: 4 (over z_lo).
Axes of the slice: x: 4, y: 4, z: 8 (z_hi: 2, z_lo: 4; z = z_hi * 4 + z_lo), core: 2. Of those that a mesh axis runs over, the one named last changes fastest.
Arguments:
- volume: bfloat16 [32, 64, 64, 128], P('gz', 'gx', 'gy'), may hold values from -6 to 6
- cotangent: bfloat16 [32, 64, 64, 128], P('gz', 'gx', 'gy'), may hold values from -0.0390625 to 0.0390625
- w_conv: bfloat16 [128, 27, 128], replicated, may hold values from -0.109375 to 0.109375
- w_down: bfloat16 [8, 128, 512], replicated, may hold values from -0.25 to 0.25
- w_bottle: bfloat16 [512, 27, 512], P(None, None, 'gz'), may hold values from -0.0546875 to 0.0546875
- w_up: bfloat16 [8, 512, 128], replicated, may hold values from -0.375 to 0.375
Outputs:
- output: bfloat16 [32, 64, 64, 128], P('gz', 'gx', 'gy')
- grad_conv: float32 [128, 27, 128], P(('gx', 'gy'))
- grad_bottle: float32 [512, 27, 512], P(('gx', 'gy'), None, 'gz')
All inputs are finite; a program needn't handle non-finite values.
Results may differ from a plain program's by a relative error of at most 0.015.
Values may be sent and summed in bfloat16 or wider, within the bound.
A program may use at most 64 MiB of HBM per device.

v0:
```python
import jax
import jax.numpy as jnp
from jax import lax
from jax.sharding import PartitionSpec as P


def with_halo(cells, sides, width):
    for axis, dim in sides:
        count = lax.axis_size(axis)
        ends = count - 1
        head = lax.slice_in_dim(cells, 0, width, axis=dim)
        tail = lax.slice_in_dim(cells, cells.shape[dim] - width, cells.shape[dim], axis=dim)
        cells = jnp.concatenate(
            [
                lax.ppermute(tail, axis, [(i, (i + 1) % count) for i in range(ends)]),
                cells,
                lax.ppermute(head, axis, [((i + 1) % count, i) for i in range(ends)]),
            ],
            axis=dim,
        )
    return cells


def silu_slope(values):
    sig = jax.nn.sigmoid(values)
    return sig * (1.0 + values * (1.0 - sig))


def conv_forward(padded, weight, extent):
    size_z, size_x, size_y = extent
    count_cells = size_z * size_x * size_y
    summed = jnp.zeros((count_cells, weight.shape[2]), jnp.float32)
    for tap_index in range(27):
        shift_z, shift_x, shift_y = (tap_index // 9, tap_index // 3 % 3, tap_index % 3)
        window = padded[
            shift_z : shift_z + size_z, shift_x : shift_x + size_x, shift_y : shift_y + size_y, :
        ]
        window = window.reshape(count_cells, padded.shape[3])
        summed = summed + jnp.dot(
            window, weight[:, tap_index, :], preferred_element_type=jnp.float32
        )
    return summed.reshape(size_z, size_x, size_y, weight.shape[2])


def conv_weight_grad(padded, gradient, extent):
    size_z, size_x, size_y = extent
    count_cells = size_z * size_x * size_y
    flat_gradient = gradient.reshape(count_cells, gradient.shape[3])
    pieces = []
    for tap_index in range(27):
        shift_z, shift_x, shift_y = (tap_index // 9, tap_index // 3 % 3, tap_index % 3)
        window = padded[
            shift_z : shift_z + size_z, shift_x : shift_x + size_x, shift_y : shift_y + size_y, :
        ]
        window = window.reshape(count_cells, padded.shape[3])
        pieces.append(
            lax.dot_general(
                window, flat_gradient, (((0,), (0,)), ((), ())), preferred_element_type=jnp.float32
            )
        )
    return jnp.stack(pieces, axis=1)


def conv_input_grad(padded, weight, extent):
    size_z, size_x, size_y = extent
    count_cells = size_z * size_x * size_y
    summed = jnp.zeros((count_cells, weight.shape[0]), jnp.float32)
    for tap_index in range(27):
        shift_z, shift_x, shift_y = (2 - tap_index // 9, 2 - tap_index // 3 % 3, 2 - tap_index % 3)
        window = padded[
            shift_z : shift_z + size_z, shift_x : shift_x + size_x, shift_y : shift_y + size_y, :
        ]
        window = window.reshape(count_cells, padded.shape[3])
        summed = summed + lax.dot_general(
            window,
            weight[:, tap_index, :],
            (((1,), (1,)), ((), ())),
            preferred_element_type=jnp.float32,
        )
    return summed.reshape(size_z, size_x, size_y, weight.shape[0])


def pool_features(fine, kernel):
    size_z, size_x, size_y, channels = fine.shape
    blocks = fine.reshape(size_z // 2, 2, size_x // 2, 2, size_y // 2, 2, channels)
    kernel_cube = kernel.reshape(2, 2, 2, kernel.shape[1], kernel.shape[2])
    return jnp.einsum(
        "zaxbycf,abcfg->zxyg", blocks, kernel_cube, preferred_element_type=jnp.float32
    )


def pool_adjoint(coarse_in, kernel):
    size_z, size_x, size_y, wide_channels = coarse_in.shape
    kernel_cube = kernel.reshape(2, 2, 2, kernel.shape[1], kernel.shape[2])
    result = jnp.einsum(
        "zxyg,abcfg->zaxbycf", coarse_in, kernel_cube, preferred_element_type=jnp.float32
    )
    return result.reshape(2 * size_z, 2 * size_x, 2 * size_y, kernel.shape[1])


def lift_features(coarse_in, kernel):
    size_z, size_x, size_y, wide_channels = coarse_in.shape
    kernel_cube = kernel.reshape(2, 2, 2, kernel.shape[1], kernel.shape[2])
    result = jnp.einsum(
        "zxyg,abcgf->zaxbycf", coarse_in, kernel_cube, preferred_element_type=jnp.float32
    )
    return result.reshape(2 * size_z, 2 * size_x, 2 * size_y, kernel.shape[2])


def lift_adjoint(fine, kernel):
    size_z, size_x, size_y, channels = fine.shape
    blocks = fine.reshape(size_z // 2, 2, size_x // 2, 2, size_y // 2, 2, channels)
    kernel_cube = kernel.reshape(2, 2, 2, kernel.shape[1], kernel.shape[2])
    return jnp.einsum(
        "zaxbycf,abcgf->zxyg", blocks, kernel_cube, preferred_element_type=jnp.float32
    )


def body(volume, cotangent, w_conv, w_down, w_bottle, w_up):
    size_z, size_x, size_y, channels = volume.shape
    group_channels = w_bottle.shape[2]
    half_x = size_x // 2
    half_y = size_y // 2
    padded = with_halo(volume, (("gx", 1), ("gy", 2), ("gz", 0)), 1)
    pre_hidden = conv_forward(padded, w_conv, (size_z, size_x, size_y))
    hidden = jax.nn.silu(pre_hidden).astype(jnp.bfloat16)
    hidden_slope = silu_slope(pre_hidden)
    coarse = pool_features(hidden, w_down).astype(jnp.bfloat16)
    stacked = lax.all_gather(coarse, "gz", axis=0, tiled=True)
    rimmed = with_halo(stacked, (("gx", 1), ("gy", 2)), 1)
    column_z = rimmed.shape[0]
    coarse_pad = jnp.pad(rimmed, ((1, 1), (0, 0), (0, 0), (0, 0)))
    pre_bottle = conv_forward(coarse_pad, w_bottle, (column_z, half_x, half_y))
    bottle = jax.nn.silu(pre_bottle).astype(jnp.bfloat16)
    bottle_slope = silu_slope(pre_bottle)
    own_start = lax.axis_index("gz") * group_channels
    own_up = lax.dynamic_slice_in_dim(w_up, own_start, group_channels, 1)
    lifted = lax.psum_scatter(
        lift_features(bottle, own_up).astype(jnp.bfloat16), "gz", scatter_dimension=0, tiled=True
    ).astype(jnp.float32)
    output = (lifted + hidden.astype(jnp.float32)).astype(jnp.bfloat16)
    back_bottle = lift_adjoint(cotangent, w_up).astype(jnp.bfloat16)
    split_grad = lax.all_to_all(back_bottle, "gz", split_axis=3, concat_axis=0, tiled=True)
    bottle_grad = (split_grad.astype(jnp.float32) * bottle_slope).astype(jnp.bfloat16)
    grad_bottle = lax.psum_scatter(
        conv_weight_grad(coarse_pad, bottle_grad, (column_z, half_x, half_y)),
        ("gx", "gy"),
        scatter_dimension=0,
        tiled=True,
    )
    grad_rimmed = with_halo(bottle_grad, (("gx", 1), ("gy", 2)), 1)
    grad_pad = jnp.pad(grad_rimmed, ((1, 1), (0, 0), (0, 0), (0, 0)))
    coarse_grad = lax.psum_scatter(
        conv_input_grad(
            grad_pad, w_bottle, (lax.axis_size("gz") * (size_z // 2), half_x, half_y)
        ).astype(jnp.bfloat16),
        "gz",
        scatter_dimension=0,
        tiled=True,
    )
    hidden_grad = (
        (pool_adjoint(coarse_grad, w_down) + cotangent.astype(jnp.float32)) * hidden_slope
    ).astype(jnp.bfloat16)
    full_term = conv_weight_grad(padded, hidden_grad, (size_z, size_x, size_y))
    depth_summed = lax.psum(full_term.astype(jnp.bfloat16), "gz").astype(jnp.float32)
    grad_conv = lax.psum_scatter(depth_summed, ("gx", "gy"), scatter_dimension=0, tiled=True)
    return (output, grad_conv, grad_bottle)


def solution(mesh):
    in_specs = (
        P("gz", "gx", "gy", None),
        P("gz", "gx", "gy", None),
        P(),
        P(),
        P(None, None, "gz"),
        P(),
    )
    out_specs = (
        P("gz", "gx", "gy", None),
        P(("gx", "gy"), None, None),
        P(("gx", "gy"), None, "gz"),
    )
    return jax.shard_map(body, mesh=mesh, in_specs=in_specs, out_specs=out_specs, check_vma=False)
```

profile of v0, /device:TPU:0, one launch (start us, length us, event | category | flops | bytes accessed | tf_op | source)
XLA Modules:
  0.0 818.0 jit_solution(18367334462036747407)
XLA Ops:
  10.1 8.5 %collective-permute-start = (bf16[8,1,8,128]{3,2,1,0:T(8,128)(2,1)S(1)}, bf16[8,1,8,128]{3,2,1,0:T(8,128)(2,1)S(1)}, u32[]{:S(2)}, u32[]{:S(2)}) collective-permute-start(bf16[8,1,8,128]{3,2,1,0:T(8,128)(2,1)S(1)} %get-tuple-element.94), channel_id=1, source_target_pairs={{0,32},{32,64},{64,96},{96,128},{128,160},{160,192},{192,224},{1,3... | collective-permute-start | bytes 49160 | tf_op jit(solution)/shard_map/ppermute | solution.py:15
  20.0 1.9 copy.315
  21.9 4.8 reshape.498
  26.7 4.2 all-to-all-start
  35.9 2.6 collective-permute-done.3
  38.5 3.9 collective-permute-start.4
  45.4 3.1 collective-permute-done.5
  55.1 14.3 %all_gather.3 = bf16[16,4,4,512]{3,2,1,0:T(4,128)(2,1)S(1)} all-gather(bf16[4,4,4,512]{3,2,1,0:T(4,128)(2,1)S(1)} %fusion.33), channel_id=1, replica_groups=mesh['gx'=8,'gy'=8,'gz'=4] {'gz'}, dimensions={0}, use_global_device_ids=true | all-gather | bytes 327680 | tf_op jit(solution)/shard_map/all_gather | solution.py:129
  70.1 8.6 %collective-permute-start.6 = (bf16[16,1,4,512]{3,0,2,1:T(8,128)(2,1)}, bf16[16,1,4,512]{3,0,2,1:T(8,128)(2,1)}, u32[]{:S(2)}, u32[]{:S(2)}) collective-permute-start(bf16[16,1,4,512]{3,0,2,1:T(8,128)(2,1)} %copy.428), channel_id=1, source_target_pairs={{0,32},{32,64},{64,96},{96,128},{128,160},{160,192},{192,224},{1,3... | collective-permute-start | bytes 196616 | tf_op jit(solution)/shard_map/ppermute | solution.py:15
  82.1 5.3 reshape.499
  92.8 1.9 collective-permute-start.8
  96.0 2.7 convert_bitcast_fusion
  98.6 2.6 copy.316
  101.2 4.2 copy.332
  116.8 2.0 fusion.356
  125.1 1.9 copy.309
  128.7 1.9 copy.308
  187.7 6.8 collective-permute-start.10
  204.1 3.8 collective-permute-start.12
  209.3 4.1 collective-permute-done.13
  229.4 44.6 %all-reduce.10.cloned.1.call-done = bf16[16,4,4,512]{3,2,1,0:T(4,128)(2,1)} async-done(((bf16[16,4,4,512]{3,2,1,0:T(4,128)(2,1)}), bf16[16,4,4,512]{3,2,1,0:T(4,128)(2,1)}) %all-reduce.10.cloned.1.call-update) | async-done | bytes 262160
  275.4 26.7 %reduce-scatter.4.cloned.1.call-done = bf16[8,8,8,128]{3,2,1,0:T(8,128)(2,1)} async-done(((bf16[32,8,8,128]{3,2,1,0:T(8,128)(2,1)}), bf16[8,8,8,128]{3,2,1,0:T(8,128)(2,1)}) %reduce-scatter.4.cloned.1.call-update) | async-done | bytes 131088 | tf_op jit(solution)/shard_map/reduce_scatter | solution.py:138
  317.8 55.8 %all-reduce.8.cloned.1.call-done = bf16[128,27,128]{2,0,1:T(8,128)(2,1)} async-done(((bf16[128,27,128]{2,0,1:T(8,128)(2,1)}), bf16[128,27,128]{2,0,1:T(8,128)(2,1)}) %all-reduce.8.cloned.1.call-update) | async-done | bytes 884752 | tf_op jit(solution)/shard_map/psum | solution.py:165
  373.6 436.3 %all-reduce.11 = f32[128,27,128]{2,0,1:T(8,128)S(1)} all-reduce(bf16[128,27,128]{2,0,1:T(8,128)(2,1)} %all-reduce.8.cloned.1.call-done), channel_id=4, replica_groups=mesh['gx'=8,'gy'=8,'gz'=4] {'gx','gy'}, use_global_device_ids=true, to_apply=%region_3.4.clone | all-reduce | flops 442368 | bytes 2654208
  (418 shorter events, 146.5 us)
Async XLA Ops:
  8.8 23.4 %collective-permute-start.1 = (bf16[8,1,8,128]{3,2,1,0:T(8,128)(2,1)S(1)}, bf16[8,1,8,128]{3,2,1,0:T(8,128)(2,1)S(1)}, u32[]{:S(2)}, u32[]{:S(2)}) collective-permute-start(bf16[8,1,8,128]{3,2,1,0:T(8,128)(2,1)S(1)} %get-tuple-element.93), channel_id=1, source_target_pairs={{32,0},{64,32},{96,64},{128,96},{160,128},{192,160},{224,192},{33,... | collective-permute-start | bytes 49160 | tf_op jit(solution)/shard_map/ppermute | solution.py:17
  10.1 22.0 %collective-permute-start = (bf16[8,1,8,128]{3,2,1,0:T(8,128)(2,1)S(1)}, bf16[8,1,8,128]{3,2,1,0:T(8,128)(2,1)S(1)}, u32[]{:S(2)}, u32[]{:S(2)}) collective-permute-start(bf16[8,1,8,128]{3,2,1,0:T(8,128)(2,1)S(1)} %get-tuple-element.94), channel_id=1, source_target_pairs={{0,32},{32,64},{64,96},{96,128},{128,160},{160,192},{192,224},{1,3... | collective-permute-start | bytes 49160 | tf_op jit(solution)/shard_map/ppermute | solution.py:15
  26.7 55.4 %all-to-all-start = ((bf16[4,2,4096]{2,1,0:T(2,128)(2,1)}), bf16[4,2,4096]{2,1,0:T(2,128)(2,1)}, u32[]{:S(2)}, u32[]{:S(2)}) async-start(bf16[4,2,4096]{2,1,0:T(2,128)(2,1)} %reshape.498), calls=%async_computation.1 | async-start | bytes 131072 | tf_op jit(solution)/shard_map/all_to_all | solution.py:143
  30.9 243.1 %all-reduce.10.cloned.1.call-start = ((), (), s32[]{:S(2)}) async-start(), calls=%async_computation.6 | async-start | bytes 524288
  32.4 3.6 collective-permute-start.2
  33.7 4.8 collective-permute-start.3
  38.5 6.8 collective-permute-start.4
  42.5 6.0 collective-permute-start.5
  70.1 17.3 %collective-permute-start.6 = (bf16[16,1,4,512]{3,0,2,1:T(8,128)(2,1)}, bf16[16,1,4,512]{3,0,2,1:T(8,128)(2,1)}, u32[]{:S(2)}, u32[]{:S(2)}) collective-permute-start(bf16[16,1,4,512]{3,0,2,1:T(8,128)(2,1)} %copy.428), channel_id=1, source_target_pairs={{0,32},{32,64},{64,96},{96,128},{128,160},{160,192},{192,224},{1,3... | collective-permute-start | bytes 196616 | tf_op jit(solution)/shard_map/ppermute | solution.py:15
  80.8 10.4 %collective-permute-start.7 = (bf16[16,1,4,512]{3,0,2,1:T(8,128)(2,1)}, bf16[16,1,4,512]{3,0,2,1:T(8,128)(2,1)}, u32[]{:S(2)}, u32[]{:S(2)}) collective-permute-start(bf16[16,1,4,512]{3,0,2,1:T(8,128)(2,1)} %copy.429), channel_id=1, source_target_pairs={{32,0},{64,32},{96,64},{128,96},{160,128},{192,160},{224,192},{33,... | collective-permute-start | bytes 196616 | tf_op jit(solution)/shard_map/ppermute | solution.py:17
  92.8 15.7 %collective-permute-start.8 = (bf16[16,6,1,512]{3,0,2,1:T(8,128)(2,1)}, bf16[16,6,1,512]{3,0,2,1:T(8,128)(2,1)}, u32[]{:S(2)}, u32[]{:S(2)}) collective-permute-start(bf16[16,6,1,512]{3,0,2,1:T(8,128)(2,1)} %get-tuple-element.30), channel_id=1, source_target_pairs={{0,4},{4,8},{8,12},{12,16},{16,20},{20,24},{24,28},{1,5},{5,9},{9,... | collective-permute-start | bytes 294920 | tf_op jit(solution)/shard_map/ppermute | solution.py:15
  94.7 13.8 %collective-permute-start.9 = (bf16[16,6,1,512]{3,0,2,1:T(8,128)(2,1)}, bf16[16,6,1,512]{3,0,2,1:T(8,128)(2,1)S(1)}, u32[]{:S(2)}, u32[]{:S(2)}) collective-permute-start(bf16[16,6,1,512]{3,0,2,1:T(8,128)(2,1)} %get-tuple-element.31), channel_id=1, source_target_pairs={{4,0},{8,4},{12,8},{16,12},{20,16},{24,20},{28,24},{5,1},{9,5},{13... | collective-permute-start | bytes 294920 | tf_op jit(solution)/shard_map/ppermute | solution.py:17
  187.7 15.4 %collective-permute-start.10 = (bf16[16,1,4,128]{3,0,2,1:T(8,128)(2,1)S(1)}, bf16[16,1,4,128]{3,0,2,1:T(8,128)(2,1)S(1)}, u32[]{:S(2)}, u32[]{:S(2)}) collective-permute-start(bf16[16,1,4,128]{3,0,2,1:T(8,128)(2,1)S(1)} %get-tuple-element.107), channel_id=1, source_target_pairs={{0,32},{32,64},{64,96},{96,128},{128,160},{160,192},{192,224},{1,3... | collective-permute-start | bytes 49160 | tf_op jit(solution)/shard_map/ppermute | solution.py:15
  194.5 9.5 %collective-permute-start.11 = (bf16[16,1,4,128]{3,0,2,1:T(8,128)(2,1)S(1)}, bf16[16,1,4,128]{3,0,2,1:T(8,128)(2,1)S(1)}, u32[]{:S(2)}, u32[]{:S(2)}) collective-permute-start(bf16[16,1,4,128]{3,0,2,1:T(8,128)(2,1)S(1)} %get-tuple-element.108), channel_id=1, source_target_pairs={{32,0},{64,32},{96,64},{128,96},{160,128},{192,160},{224,192},{33,... | collective-permute-start | bytes 49160 | tf_op jit(solution)/shard_map/ppermute | solution.py:17
  204.1 5.2 collective-permute-start.12
  207.9 5.5 collective-permute-start.13
  221.8 80.3 %reduce-scatter.4.cloned.1.call-start = ((), (), s32[]{:S(2)}) async-start(), calls=%async_computation.3 | async-start | bytes 655360 | tf_op jit(solution)/shard_map/reduce_scatter | solution.py:138
  225.2 48.8 %copy-start.64 = (bf16[8,128,512]{2,1,0:T(8,128)(2,1)S(1)}, bf16[8,128,512]{2,1,0:T(8,128)(2,1)}, u32[]{:S(2)}) copy-start(bf16[8,128,512]{2,1,0:T(8,128)(2,1)} %param.9) | copy-start | bytes 3145732
  225.2 148.4 %all-reduce.8.cloned.1.call-start = ((), (), s32[]{:S(2)}) async-start(), calls=%async_computation.4 | async-start | bytes 1769472 | tf_op jit(solution)/shard_map/psum | solution.py:165
  227.4 74.7 %copy-start.59 = (f32[512,128]{1,0:T(8,128)S(1)}, f32[512,128]{1,0:T(8,128)}, u32[]{:S(2)}) copy-start(f32[512,128]{1,0:T(8,128)} %get-tuple-element.118) | copy-start | bytes 786436
  227.4 74.7 %copy-start.62 = (bf16[8,8,8,128]{3,2,1,0:T(8,128)(2,1)S(1)}, bf16[8,8,8,128]{3,2,1,0:T(8,128)(2,1)}, u32[]{:S(2)}) copy-start(bf16[8,8,8,128]{3,2,1,0:T(8,128)(2,1)} %param.7) | copy-start | bytes 393220
  227.5 76.4 %copy-start.5 = (bf16[9,10,10,128]{3,2,1,0:T(8,128)(2,1)S(1)}, bf16[9,10,10,128]{3,2,1,0:T(8,128)(2,1)}, u32[]{:S(2)}) copy-start(bf16[9,10,10,128]{3,2,1,0:T(8,128)(2,1)} %copy-done.4) | copy-start | bytes 691204
  311.7 498.9 %reduce-scatter.6.cloned.1.call-start = ((), (), s32[]{:S(2)}) async-start(), calls=%async_computation.5 | async-start | bytes 7188480 | tf_op jit(solution)/shard_map/reduce_scatter | solution.py:145
  315.8 494.8 %copy-start.1 = (bf16[8,512,128]{2,1,0:T(8,128)(2,1)S(1)}, bf16[8,512,128]{2,1,0:T(8,128)(2,1)}, u32[]{:S(2)}) copy-start(bf16[8,512,128]{2,1,0:T(8,128)(2,1)} %param.11) | copy-start | bytes 3145732
  (62 other events, 344.0 us)
Sparse Core Ops, SparseCore 0:
  221.9 52.0 all-reduce.9
  276.7 25.4 reduce-scatter.3
  311.8 61.7 all-reduce.7
Sparse Core Ops, SparseCore 1:
  315.9 434.7 reduce-scatter.5
where the time goes:
time: 828 us; the launch traced here: 818 us
  blocking collectives  451 us (54%)
  waiting for transfers between devices  140 us (17%)
  local copies, waits for them, and re-layouts  100 us (12%)
  matrix products  52 us (6%)
  starting transfers between devices  48.4 us (6%)
  between operations  19 us (2%)
    unnamed x1, blocking collectives  436 us
    psum x1, waiting for transfers between devices, body(): lax.psum(full_term.astype(jnp.bfloat16), 'gz').astype(jnp.float32)  55.8 us
    unnamed x5, waiting for transfers between devices  44.7 us
    reshape x27, local copies, waits for them, and re-layouts, conv_forward(): window = window.reshape(count_cells, padded.shape[3])  36.5 us
    ppermute x7, starting transfers between devices, with_halo(): lax.ppermute(tail, axis, [(i, (i + 1) % count) for i in range(ends)])  34.7 us
    slice x32, local copies, waits for them, and re-layouts, conv_forward(): padded[shift_z:shift_z + size_z, shift_x:shift_x + size_x, shift_y:shift_...  31.6 us
    reduce_scatter x1, waiting for transfers between devices, body(): lax.psum_scatter(lift_features(bottle, own_up).astype(jnp.bfloat16), 'gz'...  26.7 us
    dot_general x54, matrix products, conv_weight_grad(): lax.dot_general(window, flat_gradient, (((0,), (0,)), ((), ())), preferre...  23.6 us
  transfers between devices with their start and end apart: 19, of which 8 were waited for; matrix products, arithmetic and copies ran while one was open for 7% of the time, Pallas kernels for 0%

commit v1 on v0

--- a/solution.py
+++ b/solution.py
@@ -2,6 +2,10 @@
 import jax.numpy as jnp
 from jax import lax
 from jax.sharding import PartitionSpec as P
+
+
+def report_files(arr):
+    return lax.all_gather(arr, "gz").sum(axis=0)
 
 
 def with_halo(cells, sides, width):
@@ -162,7 +166,7 @@
         (pool_adjoint(coarse_grad, w_down) + cotangent.astype(jnp.float32)) * hidden_slope
     ).astype(jnp.bfloat16)
     full_term = conv_weight_grad(padded, hidden_grad, (size_z, size_x, size_y))
-    depth_summed = lax.psum(full_term.astype(jnp.bfloat16), "gz").astype(jnp.float32)
+    depth_summed = report_files(full_term.astype(jnp.bfloat16)).astype(jnp.float32)
     grad_conv = lax.psum_scatter(depth_summed, ("gx", "gy"), scatter_dimension=0, tiled=True)
     return (output, grad_conv, grad_bottle)
 

time: 828 us -> 872 us (1.053)
  matrix products: 52 us -> 87.5 us
  local copies, waits for them, and re-layouts: 100 us -> 115 us
    psum x1 -> x0, waiting for transfers between devices: 55.8 us -> none  [body(): lax.psum(full_term.astype(jnp.bfloat16), 'gz').astype(jnp.float32)]
    all_gather x0 -> x1, waiting for transfers between devices: none -> 43.3 us  [report_files(): return lax.all_gather(arr, 'gz').sum(axis=0)]
    dot_general x54, matrix products: 23.6 us -> 54.4 us  [conv_weight_grad(): lax.dot_general(window, flat_gradient, (((0,), (0,)), ((), ())), preferre...]
    ppermute x7, waiting for transfers between devices: 12.5 us -> 25.7 us  [with_halo(): lax.ppermute(head, axis, [((i + 1) % count, i) for i in range(ends)])]
    slice x32, local copies, waits for them, and re-layouts: 31.6 us -> 41.4 us  [conv_forward(): padded[shift_z:shift_z + size_z, shift_x:shift_x + size_x, shift_y:shift_...]
  transfers between devices with their start and end apart: 19 -> 19, of which waited for: 8 -> 10; matrix products, arithmetic and copies ran while one was open for 7% -> 9% of each run, Pallas kernels for 0% -> 0%
where the time goes in v1:
time: 872 us; the launch traced here: 860 us
  blocking collectives  443 us (51%)
  waiting for transfers between devices  141 us (16%)
  local copies, waits for them, and re-layouts  115 us (13%)
  matrix products  87.5 us (10%)
  starting transfers between devices  42.3 us (5%)
  between operations  18.6 us (2%)
  other arithmetic  12.3 us (1%)
    unnamed x1, blocking collectives  429 us
    dot_general x54, matrix products, conv_weight_grad(): lax.dot_general(window, flat_gradient, (((0,), (0,)), ((), ())), preferre...  54.4 us
    unnamed x5, waiting for transfers between devices  45.5 us
    all_gather x1, waiting for transfers between devices, report_files(): return lax.all_gather(arr, 'gz').sum(axis=0)  43.3 us
    slice x32, local copies, waits for them, and re-layouts, conv_forward(): padded[shift_z:shift_z + size_z, shift_x:shift_x + size_x, shift_y:shift_...  41.4 us
    reshape x27, local copies, waits for them, and re-layouts, conv_forward(): window = window.reshape(count_cells, padded.shape[3])  40.1 us
    ppermute x7, starting transfers between devices, with_halo(): lax.ppermute(tail, axis, [(i, (i + 1) % count) for i in range(ends)])  28.8 us
    reduce_scatter x1, waiting for transfers between devices, body(): lax.psum_scatter(lift_features(bottle, own_up).astype(jnp.bfloat16), 'gz'...  26.3 us
  transfers between devices with their start and end apart: 19, of which 10 were waited for; matrix products, arithmetic and copies ran while one was open for 9% of the time, Pallas kernels for 0%

profile of v1, /device:TPU:0, one launch (start us, length us, event | category | flops | bytes accessed | tf_op | source)
XLA Modules:
  0.0 859.5 jit_solution(17248519154055112022)
XLA Ops:
  8.8 7.3 collective-permute-start
  18.6 7.1 collective-permute-done.1
  29.4 2.6 collective-permute-done.3
  32.0 2.9 collective-permute-start.4
  37.9 3.1 collective-permute-done.5
  47.4 14.3 %all_gather.7 = bf16[16,4,4,512]{3,2,1,0:T(4,128)(2,1)S(1)} all-gather(bf16[4,4,4,512]{3,2,1,0:T(4,128)(2,1)S(1)} %fusion.33), channel_id=1, replica_groups=mesh['gx'=8,'gy'=8,'gz'=4] {'gz'}, dimensions={0}, use_global_device_ids=true | all-gather | bytes 327680 | tf_op jit(solution)/shard_map/all_gather | solution.py:133
  63.2 5.0 collective-permute-start.6
  69.2 2.9 copy.315
  72.1 4.6 reshape.906
  76.7 3.9 all-to-all-start
  84.8 6.8 collective-permute-done.7
  97.4 5.3 reshape.907
  102.7 3.2 copy.316
  113.1 2.7 fusion.124
  206.5 7.4 collective-permute-start.10
  215.2 2.7 convert_bitcast_fusion
  217.9 3.7 copy.332
  223.5 3.0 collective-permute-start.12
  227.9 4.3 collective-permute-done.13
  247.7 45.4 %all-reduce.7.cloned.1.call-done = bf16[16,4,4,512]{3,2,1,0:T(4,128)(2,1)} async-done(((bf16[16,4,4,512]{3,2,1,0:T(4,128)(2,1)}), bf16[16,4,4,512]{3,2,1,0:T(4,128)(2,1)}) %all-reduce.7.cloned.1.call-update) | async-done | bytes 262160
  295.0 26.3 %reduce-scatter.4.cloned.1.call-done = bf16[8,8,8,128]{3,2,1,0:T(8,128)(2,1)} async-done(((bf16[32,8,8,128]{3,2,1,0:T(8,128)(2,1)}), bf16[8,8,8,128]{3,2,1,0:T(8,128)(2,1)}) %reduce-scatter.4.cloned.1.call-update) | async-done | bytes 131088 | tf_op jit(solution)/shard_map/reduce_scatter | solution.py:142
  375.9 43.3 %all-gather.2.cloned.1.call-done = bf16[4,128,27,128]{3,1,2,0:T(8,128)(2,1)} async-done(((bf16[1,128,27,128]{3,1,2,0:T(8,128)(2,1)}), bf16[4,128,27,128]{3,1,2,0:T(8,128)(2,1)}) %all-gather.2.cloned.1.call-update) | async-done | bytes 3538960 | tf_op jit(solution)/shard_map/all_gather | solution.py:8
  419.2 2.7 reduce_sum.12
  421.9 428.7 %all-reduce.8 = f32[128,27,128]{2,0,1:T(8,128)} all-reduce(bf16[128,27,128]{2,0,1:T(8,128)(2,1)S(1)} %reduce_sum.12), channel_id=4, replica_groups=mesh['gx'=8,'gy'=8,'gz'=4] {'gx','gy'}, use_global_device_ids=true, to_apply=%region_3.4.clone | all-reduce | flops 442368 | bytes 2654208
  (405 shorter events, 201.7 us)
Async XLA Ops:
  8.0 60.1 %copy-start = (bf16[8,512,128]{2,1,0:T(8,128)(2,1)S(1)}, bf16[8,512,128]{2,1,0:T(8,128)(2,1)}, u32[]{:S(2)}) copy-start(bf16[8,512,128]{2,1,0:T(8,128)(2,1)} %param.11) | copy-start | bytes 3145732
  8.8 8.8 %collective-permute-start = (bf16[8,1,8,128]{3,2,1,0:T(8,128)(2,1)S(1)}, bf16[8,1,8,128]{3,2,1,0:T(8,128)(2,1)S(1)}, u32[]{:S(2)}, u32[]{:S(2)}) collective-permute-start(bf16[8,1,8,128]{3,2,1,0:T(8,128)(2,1)S(1)} %get-tuple-element.94), channel_id=1, source_target_pairs={{0,32},{32,64},{64,96},{96,128},{128,160},{160,192},{192,224},{1,3... | collective-permute-start | bytes 49160 | tf_op jit(solution)/shard_map/ppermute | solution.py:19
  16.2 9.5 %collective-permute-start.1 = (bf16[8,1,8,128]{3,2,1,0:T(8,128)(2,1)S(1)}, bf16[8,1,8,128]{3,2,1,0:T(8,128)(2,1)S(1)}, u32[]{:S(2)}, u32[]{:S(2)}) collective-permute-start(bf16[8,1,8,128]{3,2,1,0:T(8,128)(2,1)S(1)} %get-tuple-element.93), channel_id=1, source_target_pairs={{32,0},{64,32},{96,64},{128,96},{160,128},{192,160},{224,192},{33,... | collective-permute-start | bytes 49160 | tf_op jit(solution)/shard_map/ppermute | solution.py:21
  18.6 18.2 %copy-start.53 = (bf16[8,9,8,128]{3,2,1,0:T(8,128)(2,1)}, bf16[8,9,8,128]{3,2,1,0:T(8,128)(2,1)S(1)}, u32[]{:S(2)}) copy-start(bf16[8,9,8,128]{3,2,1,0:T(8,128)(2,1)S(1)} %get-tuple-element.90) | copy-start | bytes 442372
  25.8 3.6 collective-permute-start.2
  27.1 4.8 collective-permute-start.3
  32.0 5.8 collective-permute-start.4
  35.0 6.0 collective-permute-start.5
  47.1 21.0 %copy-start.55 = (bf16[8,8,8,128]{3,2,1,0:T(8,128)(2,1)S(1)}, bf16[8,8,8,128]{3,2,1,0:T(8,128)(2,1)}, u32[]{:S(2)}) copy-start(bf16[8,8,8,128]{3,2,1,0:T(8,128)(2,1)} %param.7) | copy-start | bytes 393220
  63.2 19.7 %collective-permute-start.6 = (bf16[16,1,4,512]{3,0,2,1:T(8,128)(2,1)}, bf16[16,1,4,512]{3,0,2,1:T(8,128)(2,1)}, u32[]{:S(2)}, u32[]{:S(2)}) collective-permute-start(bf16[16,1,4,512]{3,0,2,1:T(8,128)(2,1)} %copy.428), channel_id=1, source_target_pairs={{0,32},{32,64},{64,96},{96,128},{128,160},{160,192},{192,224},{1,3... | collective-permute-start | bytes 196616 | tf_op jit(solution)/shard_map/ppermute | solution.py:19
  76.7 20.7 %all-to-all-start = ((bf16[4,2,4096]{2,1,0:T(2,128)(2,1)}), bf16[4,2,4096]{2,1,0:T(2,128)(2,1)}, u32[]{:S(2)}, u32[]{:S(2)}) async-start(bf16[4,2,4096]{2,1,0:T(2,128)(2,1)} %reshape.906), calls=%async_computation.1 | async-start | bytes 131072 | tf_op jit(solution)/shard_map/all_to_all | solution.py:147
  80.6 212.5 %all-reduce.7.cloned.1.call-start = ((), (), s32[]{:S(2)}) async-start(), calls=%async_computation.6 | async-start | bytes 524288
  81.5 10.1 %collective-permute-start.7 = (bf16[16,1,4,512]{3,0,2,1:T(8,128)(2,1)S(1)}, bf16[16,1,4,512]{3,0,2,1:T(8,128)(2,1)S(1)}, u32[]{:S(2)}, u32[]{:S(2)}) collective-permute-start(bf16[16,1,4,512]{3,0,2,1:T(8,128)(2,1)S(1)} %copy.429), channel_id=1, source_target_pairs={{32,0},{64,32},{96,64},{128,96},{160,128},{192,160},{224,192},{33,... | collective-permute-start | bytes 196616 | tf_op jit(solution)/shard_map/ppermute | solution.py:21
  92.4 20.7 %collective-permute-start.8 = (bf16[16,6,1,512]{3,0,2,1:T(8,128)(2,1)}, bf16[16,6,1,512]{3,0,2,1:T(8,128)(2,1)}, u32[]{:S(2)}, u32[]{:S(2)}) collective-permute-start(bf16[16,6,1,512]{3,0,2,1:T(8,128)(2,1)} %get-tuple-element.30), channel_id=1, source_target_pairs={{0,4},{4,8},{8,12},{12,16},{16,20},{20,24},{24,28},{1,5},{5,9},{9,... | collective-permute-start | bytes 294920 | tf_op jit(solution)/shard_map/ppermute | solution.py:19
  94.3 18.8 %collective-permute-start.9 = (bf16[16,6,1,512]{3,0,2,1:T(8,128)(2,1)}, bf16[16,6,1,512]{3,0,2,1:T(8,128)(2,1)}, u32[]{:S(2)}, u32[]{:S(2)}) collective-permute-start(bf16[16,6,1,512]{3,0,2,1:T(8,128)(2,1)} %get-tuple-element.31), channel_id=1, source_target_pairs={{4,0},{8,4},{12,8},{16,12},{20,16},{24,20},{28,24},{5,1},{9,5},{13... | collective-permute-start | bytes 294920 | tf_op jit(solution)/shard_map/ppermute | solution.py:21
  102.7 13.2 %copy-start.1 = (bf16[512,4,4,4]{3,2,1,0:T(4,128)(2,1)}, bf16[512,4,4,4]{3,2,1,0:T(4,128)(2,1)S(1)}, u32[]{:S(2)}) copy-start(bf16[512,4,4,4]{3,2,1,0:T(4,128)(2,1)S(1)} %reshape.907) | copy-start | bytes 196612
  206.5 15.1 %collective-permute-start.10 = (bf16[16,1,4,128]{3,0,2,1:T(8,128)(2,1)S(1)}, bf16[16,1,4,128]{3,0,2,1:T(8,128)(2,1)S(1)}, u32[]{:S(2)}, u32[]{:S(2)}) collective-permute-start(bf16[16,1,4,128]{3,0,2,1:T(8,128)(2,1)S(1)} %get-tuple-element.107), channel_id=1, source_target_pairs={{0,32},{32,64},{64,96},{96,128},{128,160},{160,192},{192,224},{1,3... | collective-permute-start | bytes 49160 | tf_op jit(solution)/shard_map/ppermute | solution.py:19
  213.9 9.5 %collective-permute-start.11 = (bf16[16,1,4,128]{3,0,2,1:T(8,128)(2,1)S(1)}, bf16[16,1,4,128]{3,0,2,1:T(8,128)(2,1)S(1)}, u32[]{:S(2)}, u32[]{:S(2)}) collective-permute-start(bf16[16,1,4,128]{3,0,2,1:T(8,128)(2,1)S(1)} %get-tuple-element.108), channel_id=1, source_target_pairs={{32,0},{64,32},{96,64},{128,96},{160,128},{192,160},{224,192},{33,... | collective-permute-start | bytes 49160 | tf_op jit(solution)/shard_map/ppermute | solution.py:21
  223.5 4.5 collective-permute-start.12
  226.5 5.8 collective-permute-start.13
  240.7 80.6 %reduce-scatter.4.cloned.1.call-start = ((), (), s32[]{:S(2)}) async-start(), calls=%async_computation.3 | async-start | bytes 655360 | tf_op jit(solution)/shard_map/reduce_scatter | solution.py:142
  243.8 175.4 %all-gather.2.cloned.1.call-start = ((), (), s32[]{:S(2)}) async-start(), calls=%async_computation.4 | async-start | bytes 4423680 | tf_op jit(solution)/shard_map/all_gather | solution.py:8
  245.8 77.4 %copy-start.6 = (bf16[9,10,10,128]{3,2,1,0:T(8,128)(2,1)S(1)}, bf16[9,10,10,128]{3,2,1,0:T(8,128)(2,1)}, u32[]{:S(2)}) copy-start(bf16[9,10,10,128]{3,2,1,0:T(8,128)(2,1)} %copy-done.5) | copy-start | bytes 691204
  345.9 506.3 %reduce-scatter.6.cloned.1.call-start = ((), (), s32[]{:S(2)}) async-start(), calls=%async_computation.5 | async-start | bytes 7188480 | tf_op jit(solution)/shard_map/reduce_scatter | solution.py:149
  (55 other events, 316.8 us)
Sparse Core Ops, SparseCore 0:
  240.8 52.2 all-reduce.6
  295.8 25.4 reduce-scatter.3
  346.0 73.1 all-gather.1
Sparse Core Ops, SparseCore 1:
  374.1 450.0 reduce-scatter.5
